TPU v7x, 256 devices: a whole 4x4x8 slice. The times are simulated.
256 devices in a mesh: gx: 8 (over z_hi, core), gy: 8 (over y, z_lo), gz: 4 (over x).
Axes of the slice: x: 4, y: 4, z: 8 (z_hi: 4, z_lo: 2; z = z_hi * 2 + z_lo), core: 2. Of those that a mesh axis runs over, the one named last changes fastest.
Arguments:
- pressure_prev: float32 [128, 192, 1024], P('gx', 'gy', 'gz'), may hold values from -6 to 6
- pressure_now: float32 [128, 192, 1024], P('gx', 'gy', 'gz'), may hold values from -6 to 6
- material: int32 [128, 192, 1024], P('gx', 'gy', 'gz'), may hold values from 0 to 7
- speed_table: float32 [8], replicated, may hold values from 0.05 to 0.32
- anchors: int32 [8, 8, 512], P('gx', 'gy', 'gz'), may hold values from 0 to 53496, as said below
- counts: int32 [8, 8, 4], P('gx', 'gy', 'gz'), may hold values from 64 to 128, as said below
- w_in: bfloat16 [512, 1024], replicated, may hold values from -0.25 to 0.25
- w_out: bfloat16 [1024, 512], replicated, may hold values from -0.1875 to 0.1875
Outputs:
- final_pressure: float32 [128, 192, 1024], P('gx', 'gy', 'gz')
- grad_in: float32 [512, 1024], P('gx')
- grad_out: float32 [1024, 512], P('gx')
Inputs may be any that keep to these rules, and one draw needn't show every extreme that they name: `anchors`: each entry is i * 24 * 256 + j * 256 + k with i <= 8, j <= 16, k <= 248, so every patch lies inside its brick; entries of a brick may repeat. The used slots of a brick are its first counts slots.
All inputs are finite; a program needn't handle non-finite values.
Results may differ from a plain program's by a relative error of at most 0.0017.
Values sent between devices are 32-bit elements; how exact they have to be, the bound alone decides.
A program may use at most 64 MiB of HBM per device.

v0:
```python
import jax
import jax.numpy as jnp
from jax import lax
from jax.sharding import PartitionSpec as P

STEPS = 8
PATCH = 8


def extended(x, sides, width):
    for axis, dim in sides:
        peers, length = (lax.axis_size(axis), x.shape[dim])
        up = [(i, (i + 1) % peers) for i in range(peers - 1)]
        down = [(j, i) for i, j in up]
        last = lax.slice_in_dim(x, length - width, length, axis=dim)
        first = lax.slice_in_dim(x, 0, width, axis=dim)
        before = lax.ppermute(last, axis, up)
        after = lax.ppermute(first, axis, down)
        x = jnp.concatenate([before, x, after], axis=dim)
    return x


def coefficient(material, speed_table):
    coef = jnp.zeros(material.shape, jnp.float32)
    for number in range(speed_table.shape[0]):
        coef = jnp.where(material == number, speed_table[number], coef)
    return coef


def update(prev, now, coef, padded):
    beside = padded[2:, 1:-1, 1:-1] + padded[:-2, 1:-1, 1:-1]
    beside = beside + padded[1:-1, 2:, 1:-1] + padded[1:-1, :-2, 1:-1]
    beside = beside + padded[1:-1, 1:-1, 2:] + padded[1:-1, 1:-1, :-2]
    return 2.0 * now - prev + coef * (beside - 6.0 * now)


def outer_sum(left, right):
    return lax.dot_general(
        left, right, (((0,), (0,)), ((), ())), preferred_element_type=jnp.float32
    )


def mlp_parts(inputs, targets, valid, total, w_in, w_out):
    scale = lax.rsqrt(jnp.mean(inputs * inputs, axis=-1, keepdims=True) + 1e-06)
    normed = (inputs * scale).astype(jnp.bfloat16)
    pre = jnp.dot(normed, w_in, preferred_element_type=jnp.float32)
    act = jax.nn.gelu(pre).astype(jnp.bfloat16)
    err = inputs + jnp.dot(act, w_out, preferred_element_type=jnp.float32) - targets
    dout = (2.0 * err * valid[:, None] / total).astype(jnp.bfloat16)
    dact = lax.dot_general(
        dout, w_out, (((1,), (1,)), ((), ())), preferred_element_type=jnp.float32
    )
    dpre = jax.vjp(jax.nn.gelu, pre)[1](dact)[0].astype(jnp.bfloat16)
    return (normed, act, dout, dpre)


def body(pressure_prev, pressure_now, material, speed_table, anchors, counts, w_in, w_out):
    coef = coefficient(material, speed_table)
    cells_x, cells_y, cells_z = pressure_now.shape
    prev, now = (pressure_prev, pressure_now)
    for step in range(STEPS):
        padded = extended(now, (("gx", 0), ("gy", 1), ("gz", 2)), 1)
        prev, now = (now, update(prev, now, coef, padded))
    local = anchors.reshape(-1)
    edge = jnp.arange(PATCH, dtype=jnp.int32)
    offsets = (
        edge[:, None, None] * (cells_y * cells_z)
        + edge[None, :, None] * cells_z
        + edge[None, None, :]
    ).reshape(-1)
    cell_index = local[:, None] + offsets[None, :]
    inputs = jnp.take(pressure_now.reshape(-1), cell_index, axis=0)
    targets = jnp.take(now.reshape(-1), cell_index, axis=0)
    slots = local.shape[0]
    used = counts.reshape(())
    total = lax.psum(used.astype(jnp.float32), ("gx", "gy", "gz"))
    valid = (jnp.arange(slots, dtype=jnp.int32) < used).astype(jnp.float32)
    normed, act, dout, dpre = mlp_parts(inputs, targets, valid, total, w_in, w_out)
    groups = lax.axis_size("gx")
    in_count = normed.shape[1] // groups
    out_count = act.shape[1] // groups
    full_in = outer_sum(normed, dpre)
    full_out = outer_sum(act, dout)
    summed_in, summed_out = lax.psum((full_in, full_out), ("gx", "gy", "gz"))
    position = lax.axis_index("gx")
    grad_in = lax.dynamic_slice_in_dim(summed_in, position * in_count, in_count, 0)
    grad_out = lax.dynamic_slice_in_dim(summed_out, position * out_count, out_count, 0)
    return (now, grad_in, grad_out)


def solution(mesh):
    return jax.shard_map(
        body,
        mesh=mesh,
        in_specs=(
            P("gx", "gy", "gz"),
            P("gx", "gy", "gz"),
            P("gx", "gy", "gz"),
            P(),
            P("gx", "gy", "gz"),
            P("gx", "gy", "gz"),
            P(),
            P(),
        ),
        out_specs=(P("gx", "gy", "gz"), P("gx", None), P("gx", None)),
        check_vma=False,
    )
```

profile of v0, /device:TPU:2, one launch (start us, length us, event | category | flops | bytes accessed | tf_op | source)
XLA Modules:
  0.0 1375.9 jit_solution(7897120378503387624)
XLA Ops:
  8.2 1.7 collective-permute-start.1
  12.3 3.8 collective-permute-done
  17.4 4.5 collective-permute-start.3
  23.6 2.4 collective-permute-start.4
  26.1 3.4 collective-permute-start.5
  30.2 3.7 collective-permute-done.4
  33.9 2.7 collective-permute-done.5
  36.6 5.7 fusion.70
  43.6 3.6 collective-permute-start.7
  49.4 5.3 collective-permute-start.9
  56.4 1.9 collective-permute-start.10
  58.4 3.9 collective-permute-start.11
  62.3 5.0 collective-permute-done.10
  67.3 1.9 collective-permute-done.11
  69.2 5.7 fusion.62
  76.2 3.3 collective-permute-start.13
  81.6 5.7 collective-permute-start.15
  87.4 1.4 collective-permute-done.15
  89.1 1.9 collective-permute-start.16
  91.0 4.0 collective-permute-start.17
  95.0 2.8 collective-permute-done.16
  97.7 1.9 collective-permute-done.17
  99.6 5.7 fusion.54
  106.6 6.7 collective-permute-start.19
  115.5 5.4 collective-permute-start.21
  122.6 1.9 collective-permute-start.22
  124.5 3.9 collective-permute-start.23
  128.4 2.8 collective-permute-done.22
  131.2 1.9 collective-permute-done.23
  133.1 5.7 fusion.46
  140.1 7.6 collective-permute-start.25
  149.9 5.4 collective-permute-start.27
  157.0 1.9 collective-permute-start.28
  158.9 3.9 collective-permute-start.29
  162.9 2.8 collective-permute-done.28
  165.6 1.9 collective-permute-done.29
  167.6 5.7 fusion.38
  174.5 7.6 collective-permute-start.31
  184.3 5.4 collective-permute-start.33
  192.1 1.9 collective-permute-start.34
  194.0 3.9 collective-permute-start.35
  198.1 2.8 collective-permute-done.34
  200.9 1.8 collective-permute-done.35
  202.7 6.6 fusion.30
  210.6 7.3 collective-permute-start.37
  220.8 6.0 collective-permute-start.39
  227.1 362.7 %gather_fusion = f32[65536]{0:T(1024)S(1)} fusion(f32[98304]{0:T(1024)S(1)} %bitcast.25, s32[65536]{0:T(1024)S(1)} %broadcast_clamp_fusion), kind=kCustom, calls=%fused_computation.clone | custom fusion | bytes 786432 | tf_op jit(solution)/shard_map/jit(_take)/gather | solution.py:72
  590.9 2.1 collective-permute-start.40
  593.0 3.9 collective-permute-start.41
  597.1 2.5 collective-permute-done.40
  599.6 1.9 collective-permute-done.41
  601.6 6.5 fusion.22
  609.4 7.9 collective-permute-start.43
  619.4 4.9 collective-permute-start.45
  627.2 1.9 collective-permute-start.46
  629.1 4.1 collective-permute-start.47
  633.2 86.1 %psum.21 = f32[]{:T(128)} all-reduce(f32[]{:T(128)S(6)} %convert_element_type.22), channel_id=1, replica_groups=mesh['gx'=8,'gy'=8,'gz'=4] {'gx','gy','gz'}, use_global_device_ids=true, to_apply=%region_1.3 | all-reduce | flops 1 | bytes 8 | tf_op jit(solution)/shard_map/psum | solution.py:76
  720.0 6.7 fusion.14
  727.0 362.7 %gather_fusion.1 = f32[65536]{0:T(1024)S(1)} fusion(f32[98304]{0:T(1024)S(1)} %bitcast.24, s32[65536]{0:T(1024)S(1)} %broadcast_clamp_fusion), kind=kCustom, calls=%fused_computation.1.clone | custom fusion | bytes 786432 | tf_op jit(solution)/shard_map/jit(_take)/gather | solution.py:73
  1090.8 1.9 fusion.94
  1092.7 2.4 fusion.75
  1095.1 270.6 %all-reduce.3.cloned.1.call-done = (f32[512,1024]{1,0:T(8,128)}, f32[1024,512]{1,0:T(8,128)}) async-done(((f32[512,1024]{1,0:T(8,128)}, f32[1024,512]{1,0:T(8,128)}), (f32[512,1024]{1,0:T(8,128)}, f32[1024,512]{1,0:T(8,128)})) %all-reduce.3.cloned.1.call-update) | async-done | bytes 4194320 | tf_op jit(solution)/shard_map/psum | solution.py:84
  1365.7 1.7 constant_dynamic-slice_fusion
  1367.3 1.7 constant_dynamic-slice_fusion.1
  (130 shorter events, 45.1 us)
Async XLA Ops:
  7.2 1082.6 %copy-start = (bf16[1024,512]{1,0:T(8,128)(2,1)S(1)}, bf16[1024,512]{1,0:T(8,128)(2,1)}, u32[]{:S(2)}) copy-start(bf16[1024,512]{1,0:T(8,128)(2,1)} %param.17) | copy-start | bytes 3145732
  7.2 29.4 %copy-start.2 = (f32[16,24,256]{2,1,0:T(8,128)S(1)}, f32[16,24,256]{2,1,0:T(8,128)}, u32[]{:S(2)}) copy-start(f32[16,24,256]{2,1,0:T(8,128)} %param.11) | copy-start | bytes 1179652
  7.2 22.3 %copy-start.12 = (f32[8]{0:T(128)S(1)}, f32[8]{0:T(128)}, u32[]{:S(2)}) copy-start(f32[8]{0:T(128)} %param.13) | copy-start | bytes 100
  7.2 29.4 %copy-start.6 = (f32[16,24,256]{2,1,0:T(8,128)S(1)}, f32[16,24,256]{2,1,0:T(8,128)}, u32[]{:S(2)}) copy-start(f32[16,24,256]{2,1,0:T(8,128)} %param.10) | copy-start | bytes 1179652
  7.2 29.4 %copy-start.1 = (s32[16,24,256]{2,1,0:T(8,128)S(1)}, s32[16,24,256]{2,1,0:T(8,128)}, u32[]{:S(2)}) copy-start(s32[16,24,256]{2,1,0:T(8,128)} %param.12) | copy-start | bytes 1179652
  7.2 1358.4 %all-reduce.3.cloned.1.call-start = ((), (), s32[]{:S(2)}) async-start(), calls=%async_computation | async-start | bytes 8388608 | tf_op jit(solution)/shard_map/psum | solution.py:84
  8.2 3.0 collective-permute-start.1
  9.9 6.1 collective-permute-start
  16.1 5.9 collective-permute-start.2
  17.4 6.0 collective-permute-start.3
  23.6 10.2 collective-permute-start.4
  26.1 10.5 collective-permute-start.5
  42.3 4.9 collective-permute-start.6
  43.6 4.4 collective-permute-start.7
  48.1 6.7 collective-permute-start.8
  49.4 6.8 collective-permute-start.9
  56.4 10.9 collective-permute-start.10
  58.4 10.9 collective-permute-start.11
  74.9 4.6 collective-permute-start.12
  76.2 4.1 collective-permute-start.13
  80.3 7.0 collective-permute-start.14
  81.6 7.2 collective-permute-start.15
  89.1 8.7 collective-permute-start.16
  91.0 8.6 collective-permute-start.17
  105.3 8.0 collective-permute-start.18
  106.6 7.5 collective-permute-start.19
  114.2 6.7 collective-permute-start.20
  115.5 6.9 collective-permute-start.21
  122.6 8.6 collective-permute-start.22
  124.5 8.6 collective-permute-start.23
  138.8 8.9 collective-permute-start.24
  140.1 8.4 collective-permute-start.25
  148.6 6.7 collective-permute-start.26
  149.9 6.9 collective-permute-start.27
  157.0 8.6 collective-permute-start.28
  158.9 8.6 collective-permute-start.29
  173.2 8.9 collective-permute-start.30
  174.5 8.5 collective-permute-start.31
  183.0 6.8 collective-permute-start.32
  184.3 6.9 collective-permute-start.33
  189.8 28.2 %copy-start.13 = (s32[1,1,128]{2,1,0:T(1,128)S(1)}, s32[1,1,128]{2,1,0:T(1,128)}, u32[]{:S(2)}) copy-start(s32[1,1,128]{2,1,0:T(1,128)} %param.14) | copy-start | bytes 1540
  192.1 8.8 collective-permute-start.34
  194.0 8.7 collective-permute-start.35
  209.3 8.8 collective-permute-start.36
  210.6 8.2 collective-permute-start.37
  218.2 8.7 copy-start.8
  218.8 8.0 copy-start.10
  219.5 370.4 %collective-permute-start.38 = (f32[18,1,256]{2,1,0:T(1,128)}, f32[18,1,256]{2,1,0:T(1,128)}, u32[]{:S(2)}, u32[]{:S(2)}) collective-permute-start(f32[18,1,256]{2,1,0:T(1,128)} %get-tuple-element.25), channel_id=1, source_target_pairs={{4,0},{8,4},{12,8},{16,12},{20,16},{24,20},{28,24},{5,1},{9,5},{13... | collective-permute-start | bytes 55304 | tf_op jit(solution)/shard_map/ppermute | solution.py:18
  220.8 369.1 %collective-permute-start.39 = (f32[18,1,256]{2,1,0:T(1,128)}, f32[18,1,256]{2,1,0:T(1,128)}, u32[]{:S(2)}, u32[]{:S(2)}) collective-permute-start(f32[18,1,256]{2,1,0:T(1,128)} %get-tuple-element.24), channel_id=1, source_target_pairs={{0,4},{4,8},{8,12},{12,16},{16,20},{20,24},{24,28},{1,5},{5,9},{9,... | collective-permute-start | bytes 55304 | tf_op jit(solution)/shard_map/ppermute | solution.py:17
  227.1 362.8 %copy-start.9 = (f32[1,24,256]{2,1,0:T(8,128)S(1)}, f32[1,24,256]{2,1,0:T(8,128)}, u32[]{:S(2)}) copy-start(f32[1,24,256]{2,1,0:T(8,128)} %copy-done.8) | copy-start | bytes 73732
  227.1 362.8 %copy-start.11 = (f32[1,24,256]{2,1,0:T(8,128)S(1)}, f32[1,24,256]{2,1,0:T(8,128)}, u32[]{:S(2)}) copy-start(f32[1,24,256]{2,1,0:T(8,128)} %copy-done.10) | copy-start | bytes 73732
  590.7 33.6 %copy-start.5 = (bf16[512,1024]{1,0:T(8,128)(2,1)S(1)}, bf16[512,1024]{1,0:T(8,128)(2,1)}, u32[]{:S(2)}) copy-start(bf16[512,1024]{1,0:T(8,128)(2,1)} %param.16) | copy-start | bytes 3145732
  590.9 8.7 collective-permute-start.40
  593.0 8.6 collective-permute-start.41
  608.1 9.2 collective-permute-start.42
  609.4 8.8 collective-permute-start.43
  618.1 8.0 collective-permute-start.44
  619.4 6.7 collective-permute-start.45
  627.2 92.1 %collective-permute-start.46 = (f32[18,26,1]{2,1,0:T(8,128)}, f32[18,26,1]{2,1,0:T(8,128)S(1)}, u32[]{:S(2)}, u32[]{:S(2)}) collective-permute-start(f32[18,26,1]{2,1,0:T(8,128)} %get-tuple-element.6), channel_id=1, source_target_pairs={{1,0},{2,1},{3,2},{5,4},{6,5},{7,6},{9,8},{10,9},{11,10},{13,12},{... | collective-permute-start | bytes 5624 | tf_op jit(solution)/shard_map/ppermute | solution.py:18
  629.1 90.9 %collective-permute-start.47 = (f32[18,26,1]{2,1,0:T(8,128)}, f32[18,26,1]{2,1,0:T(8,128)}, u32[]{:S(2)}, u32[]{:S(2)}) collective-permute-start(f32[18,26,1]{2,1,0:T(8,128)} %get-tuple-element.7), channel_id=1, source_target_pairs={{0,1},{1,2},{2,3},{4,5},{5,6},{6,7},{8,9},{9,10},{10,11},{12,13},{... | collective-permute-start | bytes 5624 | tf_op jit(solution)/shard_map/ppermute | solution.py:17
  719.3 0.7 copy-start.7
  726.7 362.9 %copy-start.4 = (f32[16,24,256]{2,1,0:T(8,128)}, f32[16,24,256]{2,1,0:T(8,128)S(1)}, u32[]{:S(2)}) copy-start(f32[16,24,256]{2,1,0:T(8,128)S(1)} %fusion.14) | copy-start | bytes 1179652
  726.9 362.8 %copy-start.3 = (f32[128,1024]{1,0:T(8,128)S(1)}, f32[128,1024]{1,0:T(8,128)}, u32[]{:S(2)}) copy-start(f32[128,1024]{1,0:T(8,128)} %fusion.93) | copy-start | bytes 1572868
Sparse Core Ops, SparseCore 0:
  1095.2 270.4 all-reduce.2
where the time goes:
time: 1380 us
  local copies, waits for them, and re-layouts  735 us (53%)
  waiting for transfers between devices  325 us (24%)
  starting transfers between devices  156 us (11%)
  blocking collectives  86.1 us (6%)
  other arithmetic  50.9 us (4%)
  between operations  15.7 us (1%)
    gather x2, local copies, waits for them, and re-layouts, body(): targets = jnp.take(now.reshape(-1), cell_index, axis=0)  363 us
    gather x2, local copies, waits for them, and re-layouts, body(): inputs = jnp.take(pressure_now.reshape(-1), cell_index, axis=0)  363 us
    psum x1, waiting for transfers between devices, body(): summed_in, summed_out = lax.psum((full_in, full_out), ('gx', 'gy', 'gz'))  271 us
    ppermute x24, starting transfers between devices, extended(): before = lax.ppermute(last, axis, up)  120 us
    psum x1, blocking collectives, body(): total = lax.psum(used.astype(jnp.float32), ('gx', 'gy', 'gz'))  86.1 us
    add x8, other arithmetic, update(): return 2.0 * now - prev + coef * (beside - 6.0 * now)  48.1 us
    ppermute x24, starting transfers between devices, extended(): after = lax.ppermute(first, axis, down)  36.7 us
    ppermute x24, waiting for transfers between devices, extended(): before = lax.ppermute(last, axis, up)  28.2 us
  transfers between devices with their start and end apart: 49, of which 29 were waited for; matrix products, arithmetic and copies ran while one was open for 27% of the time, Pallas kernels for 0%

commit v1 on v0

--- a/solution.py
+++ b/solution.py
@@ -81,7 +81,7 @@
     out_count = act.shape[1] // groups
     full_in = outer_sum(normed, dpre)
     full_out = outer_sum(act, dout)
-    summed_in, summed_out = lax.psum((full_in, full_out), ("gx", "gy", "gz"))
+    summed_in, summed_out = lax.psum(lax.psum((full_in, full_out), "gx"), ("gy", "gz"))
     position = lax.axis_index("gx")
     grad_in = lax.dynamic_slice_in_dim(summed_in, position * in_count, in_count, 0)
     grad_out = lax.dynamic_slice_in_dim(summed_out, position * out_count, out_count, 0)

time: 1380 us -> 1550 us (1.12)
  waiting for transfers between devices: 325 us -> 500 us
    psum x1 -> x2, waiting for transfers between devices: 271 us -> 445 us  [the longest x1 329 us: body(): lax.psum(lax.psum((full_in, full_out), 'gx'), ('gy', 'gz'))]
  transfers between devices with their start and end apart: 49 -> 50, of which waited for: 29 -> 30; matrix products, arithmetic and copies ran while one was open for 27% -> 24% of each run, Pallas kernels for 0% -> 0%
where the time goes in v1:
time: 1550 us
  local copies, waits for them, and re-layouts  735 us (47%)
  waiting for transfers between devices  500 us (32%)
  starting transfers between devices  156 us (10%)
  blocking collectives  86.1 us (6%)
  other arithmetic  49.8 us (3%)
  between operations  15.7 us (1%)
    gather x2, local copies, waits for them, and re-layouts, body(): inputs = jnp.take(pressure_now.reshape(-1), cell_index, axis=0)  363 us
    gather x2, local copies, waits for them, and re-layouts, body(): targets = jnp.take(now.reshape(-1), cell_index, axis=0)  363 us
    psum x1, waiting for transfers between devices, body(): lax.psum(lax.psum((full_in, full_out), 'gx'), ('gy', 'gz'))  329 us
    ppermute x24, starting transfers between devices, extended(): before = lax.ppermute(last, axis, up)  120 us
    psum x1, waiting for transfers between devices, body(): lax.psum((full_in, full_out), 'gx')  116 us
    psum x1, blocking collectives, body(): total = lax.psum(used.astype(jnp.float32), ('gx', 'gy', 'gz'))  86.1 us
    add x8, other arithmetic, update(): return 2.0 * now - prev + coef * (beside - 6.0 * now)  47 us
    ppermute x24, starting transfers between devices, extended(): after = lax.ppermute(first, axis, down)  36.7 us
  transfers between devices with their start and end apart: 50, of which 30 were waited for; matrix products, arithmetic and copies ran while one was open for 24% of the time, Pallas kernels for 0%

profile of v1, /device:TPU:2, one launch (start us, length us, event | category | flops | bytes accessed | tf_op | source)
XLA Modules:
  0.0 1549.6 jit_solution(10346805802894425387)
XLA Ops:
  8.2 1.7 collective-permute-start.1
  12.3 3.8 collective-permute-done
  17.4 4.5 collective-permute-start.3
  23.6 2.4 collective-permute-start.4
  26.1 3.4 collective-permute-start.5
  30.2 3.7 collective-permute-done.4
  33.9 2.7 collective-permute-done.5
  36.6 5.5 fusion.70
  43.5 3.6 collective-permute-start.7
  49.2 5.3 collective-permute-start.9
  56.3 1.9 collective-permute-start.10
  58.2 3.9 collective-permute-start.11
  62.2 5.0 collective-permute-done.10
  67.2 1.9 collective-permute-done.11
  69.1 5.5 fusion.62
  75.9 3.3 collective-permute-start.13
  81.4 5.7 collective-permute-start.15
  88.8 1.9 collective-permute-start.16
  90.7 4.0 collective-permute-start.17
  94.7 2.8 collective-permute-done.16
  97.5 1.9 collective-permute-done.17
  99.4 5.5 fusion.54
  106.2 6.7 collective-permute-start.19
  115.1 5.4 collective-permute-start.21
  122.2 1.9 collective-permute-start.22
  124.1 3.9 collective-permute-start.23
  128.1 2.8 collective-permute-done.22
  130.8 1.9 collective-permute-done.23
  132.7 5.5 fusion.46
  139.6 7.6 collective-permute-start.25
  149.4 5.4 collective-permute-start.27
  156.5 1.9 collective-permute-start.28
  158.4 3.9 collective-permute-start.29
  162.4 2.8 collective-permute-done.28
  165.1 1.9 collective-permute-done.29
  167.0 5.5 fusion.38
  173.9 7.6 collective-permute-start.31
  183.7 5.4 collective-permute-start.33
  191.4 1.9 collective-permute-start.34
  193.4 3.9 collective-permute-start.35
  197.5 2.8 collective-permute-done.34
  200.3 1.8 collective-permute-done.35
  202.1 6.5 fusion.30
  209.9 7.3 collective-permute-start.37
  220.0 6.0 collective-permute-start.39
  226.3 362.7 %gather_fusion = f32[65536]{0:T(1024)S(1)} fusion(f32[98304]{0:T(1024)S(1)} %bitcast.25, s32[65536]{0:T(1024)S(1)} %broadcast_clamp_fusion), kind=kCustom, calls=%fused_computation.clone | custom fusion | bytes 786432 | tf_op jit(solution)/shard_map/jit(_take)/gather | solution.py:72
  590.1 2.1 collective-permute-start.40
  592.2 3.9 collective-permute-start.41
  596.3 2.5 collective-permute-done.40
  598.9 1.9 collective-permute-done.41
  600.8 6.3 fusion.22
  608.5 7.9 collective-permute-start.43
  618.5 4.8 collective-permute-start.45
  626.3 1.9 collective-permute-start.46
  628.2 4.1 collective-permute-start.47
  632.3 86.1 %psum.35 = f32[]{:T(128)} all-reduce(f32[]{:T(128)S(6)} %convert_element_type.22), channel_id=1, replica_groups=mesh['gx'=8,'gy'=8,'gz'=4] {'gx','gy','gz'}, use_global_device_ids=true, to_apply=%region_1.3 | all-reduce | flops 1 | bytes 8 | tf_op jit(solution)/shard_map/psum | solution.py:76
  719.1 6.5 fusion.14
  725.9 362.7 %gather_fusion.1 = f32[65536]{0:T(1024)S(1)} fusion(f32[98304]{0:T(1024)S(1)} %bitcast.24, s32[65536]{0:T(1024)S(1)} %broadcast_clamp_fusion), kind=kCustom, calls=%fused_computation.1.clone | custom fusion | bytes 786432 | tf_op jit(solution)/shard_map/jit(_take)/gather | solution.py:73
  1089.7 1.9 fusion.94
  1091.6 2.4 fusion.75
  1094.1 116.4 %all-reduce.7.cloned.1.call-done = (f32[512,1024]{1,0:T(8,128)}, f32[1024,512]{1,0:T(8,128)}) async-done(((f32[512,1024]{1,0:T(8,128)}, f32[1024,512]{1,0:T(8,128)}), (f32[512,1024]{1,0:T(8,128)}, f32[1024,512]{1,0:T(8,128)})) %all-reduce.7.cloned.1.call-update) | async-done | bytes 4194320 | tf_op jit(solution)/shard_map/psum | solution.py:84
  1210.5 328.9 %all-reduce.5.cloned.1.call-done = (f32[512,1024]{1,0:T(8,128)}, f32[1024,512]{1,0:T(8,128)}) async-done(((f32[512,1024]{1,0:T(8,128)}, f32[1024,512]{1,0:T(8,128)}), (f32[512,1024]{1,0:T(8,128)}, f32[1024,512]{1,0:T(8,128)})) %all-reduce.5.cloned.1.call-update) | async-done | bytes 4194320 | tf_op jit(solution)/shard_map/psum | solution.py:84
  1539.4 1.7 constant_dynamic-slice_fusion
  1541.1 1.7 constant_dynamic-slice_fusion.1
  (133 shorter events, 46.5 us)
Async XLA Ops:
  7.2 1081.5 %copy-start = (bf16[1024,512]{1,0:T(8,128)(2,1)S(1)}, bf16[1024,512]{1,0:T(8,128)(2,1)}, u32[]{:S(2)}) copy-start(bf16[1024,512]{1,0:T(8,128)(2,1)} %param.17) | copy-start | bytes 3145732
  7.2 29.4 %copy-start.2 = (f32[16,24,256]{2,1,0:T(8,128)S(1)}, f32[16,24,256]{2,1,0:T(8,128)}, u32[]{:S(2)}) copy-start(f32[16,24,256]{2,1,0:T(8,128)} %param.11) | copy-start | bytes 1179652
  7.2 22.3 %copy-start.12 = (f32[8]{0:T(128)S(1)}, f32[8]{0:T(128)}, u32[]{:S(2)}) copy-start(f32[8]{0:T(128)} %param.13) | copy-start | bytes 100
  7.2 29.4 %copy-start.6 = (f32[16,24,256]{2,1,0:T(8,128)S(1)}, f32[16,24,256]{2,1,0:T(8,128)}, u32[]{:S(2)}) copy-start(f32[16,24,256]{2,1,0:T(8,128)} %param.10) | copy-start | bytes 1179652
  7.2 29.4 %copy-start.1 = (s32[16,24,256]{2,1,0:T(8,128)S(1)}, s32[16,24,256]{2,1,0:T(8,128)}, u32[]{:S(2)}) copy-start(s32[16,24,256]{2,1,0:T(8,128)} %param.12) | copy-start | bytes 1179652
  7.2 1203.3 %all-reduce.7.cloned.1.call-start = ((), (), s32[]{:S(2)}) async-start(), calls=%async_computation.1 | async-start | bytes 8388608 | tf_op jit(solution)/shard_map/psum | solution.py:84
  8.2 3.0 collective-permute-start.1
  9.9 6.1 collective-permute-start
  16.1 5.9 collective-permute-start.2
  17.4 6.0 collective-permute-start.3
  23.6 10.2 collective-permute-start.4
  26.1 10.5 collective-permute-start.5
  42.2 4.9 collective-permute-start.6
  43.5 4.4 collective-permute-start.7
  47.9 6.7 collective-permute-start.8
  49.2 6.8 collective-permute-start.9
  56.3 10.9 collective-permute-start.10
  58.2 10.9 collective-permute-start.11
  74.6 4.6 collective-permute-start.12
  75.9 4.1 collective-permute-start.13
  80.1 7.0 collective-permute-start.14
  81.4 7.2 collective-permute-start.15
  88.8 8.7 collective-permute-start.16
  90.7 8.6 collective-permute-start.17
  104.9 8.0 collective-permute-start.18
  106.2 7.5 collective-permute-start.19
  113.8 6.7 collective-permute-start.20
  115.1 6.9 collective-permute-start.21
  122.2 8.6 collective-permute-start.22
  124.1 8.6 collective-permute-start.23
  138.3 8.9 collective-permute-start.24
  139.6 8.4 collective-permute-start.25
  148.1 6.7 collective-permute-start.26
  149.4 6.9 collective-permute-start.27
  156.5 8.6 collective-permute-start.28
  158.4 8.6 collective-permute-start.29
  172.6 8.9 collective-permute-start.30
  173.9 8.5 collective-permute-start.31
  182.4 6.8 collective-permute-start.32
  183.7 6.9 collective-permute-start.33
  189.2 28.0 %copy-start.13 = (s32[1,1,128]{2,1,0:T(1,128)S(1)}, s32[1,1,128]{2,1,0:T(1,128)}, u32[]{:S(2)}) copy-start(s32[1,1,128]{2,1,0:T(1,128)} %param.14) | copy-start | bytes 1540
  191.4 8.8 collective-permute-start.34
  193.4 8.7 collective-permute-start.35
  208.6 8.8 collective-permute-start.36
  209.9 8.2 collective-permute-start.37
  217.4 8.6 copy-start.8
  218.0 8.0 copy-start.10
  218.7 370.4 %collective-permute-start.38 = (f32[18,1,256]{2,1,0:T(1,128)}, f32[18,1,256]{2,1,0:T(1,128)}, u32[]{:S(2)}, u32[]{:S(2)}) collective-permute-start(f32[18,1,256]{2,1,0:T(1,128)} %get-tuple-element.27), channel_id=1, source_target_pairs={{4,0},{8,4},{12,8},{16,12},{20,16},{24,20},{28,24},{5,1},{9,5},{13... | collective-permute-start | bytes 55304 | tf_op jit(solution)/shard_map/ppermute | solution.py:18
  220.0 369.1 %collective-permute-start.39 = (f32[18,1,256]{2,1,0:T(1,128)}, f32[18,1,256]{2,1,0:T(1,128)}, u32[]{:S(2)}, u32[]{:S(2)}) collective-permute-start(f32[18,1,256]{2,1,0:T(1,128)} %get-tuple-element.26), channel_id=1, source_target_pairs={{0,4},{4,8},{8,12},{12,16},{16,20},{20,24},{24,28},{1,5},{5,9},{9,... | collective-permute-start | bytes 55304 | tf_op jit(solution)/shard_map/ppermute | solution.py:17
  226.3 362.8 %copy-start.9 = (f32[1,24,256]{2,1,0:T(8,128)S(1)}, f32[1,24,256]{2,1,0:T(8,128)}, u32[]{:S(2)}) copy-start(f32[1,24,256]{2,1,0:T(8,128)} %copy-done.8) | copy-start | bytes 73732
  226.3 362.8 %copy-start.11 = (f32[1,24,256]{2,1,0:T(8,128)S(1)}, f32[1,24,256]{2,1,0:T(8,128)}, u32[]{:S(2)}) copy-start(f32[1,24,256]{2,1,0:T(8,128)} %copy-done.10) | copy-start | bytes 73732
  590.0 33.4 %copy-start.5 = (bf16[512,1024]{1,0:T(8,128)(2,1)S(1)}, bf16[512,1024]{1,0:T(8,128)(2,1)}, u32[]{:S(2)}) copy-start(bf16[512,1024]{1,0:T(8,128)(2,1)} %param.16) | copy-start | bytes 3145732
  590.1 8.7 collective-permute-start.40
  592.2 8.6 collective-permute-start.41
  607.2 9.2 collective-permute-start.42
  608.5 8.8 collective-permute-start.43
  617.2 8.0 collective-permute-start.44
  618.5 6.7 collective-permute-start.45
  626.3 92.1 %collective-permute-start.46 = (f32[18,26,1]{2,1,0:T(8,128)}, f32[18,26,1]{2,1,0:T(8,128)S(1)}, u32[]{:S(2)}, u32[]{:S(2)}) collective-permute-start(f32[18,26,1]{2,1,0:T(8,128)} %get-tuple-element.8), channel_id=1, source_target_pairs={{1,0},{2,1},{3,2},{5,4},{6,5},{7,6},{9,8},{10,9},{11,10},{13,12},{... | collective-permute-start | bytes 5624 | tf_op jit(solution)/shard_map/ppermute | solution.py:18
  628.2 91.0 %collective-permute-start.47 = (f32[18,26,1]{2,1,0:T(8,128)}, f32[18,26,1]{2,1,0:T(8,128)}, u32[]{:S(2)}, u32[]{:S(2)}) collective-permute-start(f32[18,26,1]{2,1,0:T(8,128)} %get-tuple-element.9), channel_id=1, source_target_pairs={{0,1},{1,2},{2,3},{4,5},{5,6},{6,7},{8,9},{9,10},{10,11},{12,13},{... | collective-permute-start | bytes 5624 | tf_op jit(solution)/shard_map/ppermute | solution.py:17
  718.4 0.7 copy-start.7
  725.7 362.9 %copy-start.4 = (f32[16,24,256]{2,1,0:T(8,128)}, f32[16,24,256]{2,1,0:T(8,128)S(1)}, u32[]{:S(2)}) copy-start(f32[16,24,256]{2,1,0:T(8,128)S(1)} %fusion.14) | copy-start | bytes 1179652
  725.9 362.8 %copy-start.3 = (f32[128,1024]{1,0:T(8,128)S(1)}, f32[128,1024]{1,0:T(8,128)}, u32[]{:S(2)}) copy-start(f32[128,1024]{1,0:T(8,128)} %fusion.93) | copy-start | bytes 1572868
  1094.0 445.4 %all-reduce.5.cloned.1.call-start = ((), (), s32[]{:S(2)}) async-start(), calls=%async_computation | async-start | bytes 8388608 | tf_op jit(solution)/shard_map/psum | solution.py:84
Sparse Core Ops, SparseCore 0:
  1094.1 116.2 all-reduce.6
  1213.2 326.1 all-reduce.4
